TPU v7x, 32 devices: a whole 2x2x4 slice. The times are simulated.
32 devices in a mesh: blk: 16 (over z, y, x), tok: 2 (over core).
Axes of the slice: x: 2, y: 2, z: 4, core: 2. Of those that a mesh axis runs over, the one named last changes fastest.
Arguments:
- tokens: bfloat16 [512, 9216], P(('tok', 'blk')), parts along dimension 0, may hold values from -6 to 6
- block_ids: int32 [512, 2], P(('tok', 'blk')), parts along dimension 0, may hold values from 0 to 15, all different within a row; in each aligned block of 16 rows (0 to 15, 16 to 31, ...) at most 5 rows name the same one
- w_in: bfloat16 [9216, 2048], P(None, 'blk'), may hold values from -0.0625 to 0.0625
- bias_in: float32 [2048], P('blk'), may hold values from -3 to 3
- w_out: bfloat16 [2048, 9216], P('blk'), may hold values from -0.375 to 0.375
Outputs:
- ffn_out: bfloat16 [512, 9216], P(('tok', 'blk')), parts along dimension 0
There are 2 independent parts, one for each index of `tok`. A program takes and returns all parts, laid end to end along the dimension named above; an argument that names none is the same for every part. Nothing has to cross between parts.
Inputs may be any that keep to these rules, and one draw needn't show every extreme that they name: `block_ids`: each row names 2 different blocks. Among the 16 rows of one device no block is named by more than 5 rows, and some block is named by exactly 5 of them.
All inputs are finite; a program needn't handle non-finite values.
Results may differ from a plain program's by a relative error of at most 0.0057.
Values may be sent and summed in bfloat16 or wider, within the bound.
A program may use at most 128 MiB of HBM per device.

v0:
```python
import jax
import jax.numpy as jnp
from jax import lax
from jax.sharding import PartitionSpec as P

CAP = 5


def body(tokens, block_ids, w_in, bias_in, w_out):
    tok_dev = tokens.shape[0]
    model_width = tokens.shape[1]
    peer_count = lax.axis_size("blk")
    top_count = block_ids.shape[1]
    slot_total = peer_count * CAP
    flat_ids = block_ids.reshape(-1)
    onehot = (flat_ids[:, None] == jnp.arange(peer_count, dtype=jnp.int32)[None, :]).astype(
        jnp.int32
    )
    before = jnp.cumsum(onehot, axis=0) - onehot
    position = jnp.sum(before * onehot, axis=1)
    slot_index = (flat_ids * CAP + position).reshape(tok_dev, top_count)
    slot_range = jnp.arange(slot_total, dtype=jnp.int32)
    routing = jnp.any(slot_index[:, :, None] == slot_range[None, None, :], axis=1).astype(
        jnp.bfloat16
    )
    outgoing = jnp.dot(routing.T, tokens, preferred_element_type=jnp.float32).astype(jnp.bfloat16)
    outgoing = outgoing.reshape(peer_count, CAP, model_width)
    incoming = lax.all_to_all(outgoing, "blk", split_axis=0, concat_axis=0, tiled=True)
    shape_in = incoming.shape
    flat_rows = incoming.reshape(-1, model_width)
    pre_act = jnp.dot(flat_rows, w_in, preferred_element_type=jnp.float32) + bias_in[None, :]
    hidden = jnp.maximum(pre_act, 0.0).astype(jnp.bfloat16)
    result = jnp.dot(hidden, w_out, preferred_element_type=jnp.float32).astype(jnp.bfloat16)
    partial_value = result.reshape(shape_in)
    returned = lax.all_to_all(partial_value, "blk", split_axis=0, concat_axis=0, tiled=True)
    returned = returned.reshape(slot_total, model_width)
    combined = jnp.dot(routing, returned, preferred_element_type=jnp.float32)
    return combined.astype(jnp.bfloat16)


def solution(mesh):
    return jax.shard_map(
        body,
        mesh=mesh,
        in_specs=(
            P(("tok", "blk"), None),
            P(("tok", "blk"), None),
            P(None, "blk"),
            P("blk"),
            P("blk", None),
        ),
        out_specs=P(("tok", "blk"), None),
        check_vma=False,
    )
```

profile of v0, /device:TPU:0, one launch (start us, length us, event | category | flops | bytes accessed | tf_op | source)
XLA Modules:
  0.0 144.7 jit_solution(14772252286774880687)
XLA Ops:
  0.0 0.0 copy-start
  0.0 0.9 copy.16
  0.9 0.1 eq.28
  1.0 0.1 fusion.4
  1.1 0.1 reduce_window_sum.11
  1.1 0.2 select_reduce_fusion
  1.3 0.1 reduce_sum.12
  1.4 0.1 copy.17
  1.5 0.7 multiply_add_fusion
  2.2 0.1 fusion.5
  2.3 2.7 %convolution_convert_fusion.1 = bf16[80,9216]{1,0:T(8,128)(2,1)} fusion(pred[16,80]{1,0:T(8,128)(4,1)S(1)} %fusion.5, bf16[16,9216]{1,0:T(8,128)(2,1)} %param.5), kind=kOutput, calls=%fused_computation.1 | convolution fusion | flops 24330240 | bytes 1770752 | tf_op jit(solution)/shard_map/dot_general | solution.py:26
  4.9 2.9 %reshape.21 = bf16[16,5,9216]{2,1,0:T(8,128)(2,1)} reshape(bf16[80,9216]{1,0:T(8,128)(2,1)} %convolution_convert_fusion.1) | data formatting | bytes 2949120 | tf_op jit(solution)/shard_map/reshape | solution.py:27
  7.8 63.4 %all_to_all.10 = bf16[16,5,9216]{2,1,0:T(8,128)(2,1)} all-to-all(bf16[16,5,9216]{2,1,0:T(8,128)(2,1)} %reshape.21), channel_id=1, replica_groups=mesh['blk'=16,'tok'=2] {'blk'}, dimensions={0} | all-to-all | bytes 2949120 | tf_op jit(solution)/shard_map/all_to_all | solution.py:28
  71.2 0.0 copy-start.1
  71.2 2.9 %reshape.22 = bf16[80,9216]{1,0:T(8,128)(2,1)} reshape(bf16[16,5,9216]{2,1,0:T(8,128)(2,1)} %all_to_all.10) | data formatting | bytes 2949120 | tf_op jit(solution)/shard_map/reshape | solution.py:30
  74.1 0.0 copy-done
  74.1 0.0 copy-done.1
  74.1 4.3 %convolution_convert_fusion = bf16[80,9216]{1,0:T(8,128)(2,1)} fusion(bf16[128,9216]{1,0:T(8,128)(2,1)S(1)} %copy-done, bf16[80,9216]{1,0:T(8,128)(2,1)} %reshape.22, bf16[9216,128]{1,0:T(8,128)(2,1)} %param.7, f32[128]{0:T(128)S(1)} %copy-done.1), kind=kOutput, calls=%fused_computation | convolution fusion | flops 378255360 | bytes 7668224 | tf_op jit(solution)/shard_map/dot_general | solution.py:33
  78.4 2.9 %reshape.23 = bf16[16,5,9216]{2,1,0:T(8,128)(2,1)} reshape(bf16[80,9216]{1,0:T(8,128)(2,1)} %convolution_convert_fusion) | data formatting | bytes 2949120 | tf_op jit(solution)/shard_map/reshape | solution.py:34
  81.3 58.2 %all_to_all.11 = bf16[16,5,9216]{2,1,0:T(8,128)(2,1)} all-to-all(bf16[16,5,9216]{2,1,0:T(8,128)(2,1)} %reshape.23), channel_id=1, replica_groups=mesh['blk'=16,'tok'=2] {'blk'}, dimensions={0} | all-to-all | bytes 2949120 | tf_op jit(solution)/shard_map/all_to_all | solution.py:35
  139.5 2.8 %reshape.24 = bf16[80,9216]{1,0:T(8,128)(2,1)} reshape(bf16[16,5,9216]{2,1,0:T(8,128)(2,1)} %all_to_all.11) | data formatting | bytes 2949120 | tf_op jit(solution)/shard_map/reshape | solution.py:36
  142.3 2.4 %convolution_convert_fusion.2 = bf16[16,9216]{1,0:T(8,128)(2,1)} fusion(pred[16,80]{1,0:T(8,128)(4,1)S(1)} %fusion.5, bf16[80,9216]{1,0:T(8,128)(2,1)} %reshape.24), kind=kOutput, calls=%fused_computation.2 | convolution fusion | flops 23740416 | bytes 1770752 | tf_op jit(solution)/shard_map/dot_general | solution.py:37
Async XLA Ops:
  0.0 74.1 %copy-start = (bf16[128,9216]{1,0:T(8,128)(2,1)S(1)}, bf16[128,9216]{1,0:T(8,128)(2,1)}, u32[]{:S(2)}) copy-start(bf16[128,9216]{1,0:T(8,128)(2,1)} %param.9) | copy-start | bytes 7077892
  71.2 2.9 %copy-start.1 = (f32[128]{0:T(128)S(1)}, f32[128]{0:T(128)}, u32[]{:S(2)}) copy-start(f32[128]{0:T(128)} %param.8) | copy-start | bytes 1540
where the time goes:
time: 145 us
  blocking collectives  122 us (84%)
  local copies, waits for them, and re-layouts  12.6 us (9%)
  matrix products  9.4 us (6%)
    all_to_all x1, blocking collectives, body(): lax.all_to_all(outgoing, 'blk', split_axis=0, concat_axis=0, tiled=True)  63.4 us
    all_to_all x1, blocking collectives, body(): lax.all_to_all(partial_value, 'blk', split_axis=0, concat_axis=0, tiled=T...  58.2 us
    dot_general x1, matrix products, body(): jnp.dot(hidden, w_out, preferred_element_type=jnp.float32)  4.33 us

commit v1 on v0

v1 whole, which is shorter than its diff:
```python
import functools
import math

import jax
import jax.numpy as jnp
from jax import lax
from jax.experimental import pallas as pl
from jax.experimental.pallas import tpu as pltpu
from jax.sharding import PartitionSpec as P

CAP = 5
PARTS = 8
F32 = jnp.float32
BF16 = jnp.bfloat16


def iota(shape, dim):
    return lax.broadcasted_iota(jnp.int32, shape, dim)


def kernel(
    n, group, tok_ref, ids_ref, w_in_ref, bias_ref, w_out_ref, out_ref,
    tok8, win8, wout8, outgoing, incoming, result, returned, route, acc,
    load_sem, fsend, frecv, bsend, brecv,
):
    me = lax.axis_index("blk")
    tok_dev, top = ids_ref.shape
    width = tok8.shape[1]
    neurons = w_in_ref.shape[1]
    lanes = 128 * ((n + 127) // 128)
    slab = CAP * PARTS
    rows = group * slab

    loads = []
    for h in range(PARTS):
        cols = pl.ds(h * width, width)
        loads.append(pltpu.make_async_copy(
            tok_ref.at[:, cols], tok8.at[pl.ds(h * tok_dev, tok_dev)], load_sem.at[0, h]))
        loads.append(pltpu.make_async_copy(
            w_in_ref.at[cols], win8.at[:, pl.ds(h * neurons, neurons)], load_sem.at[1, h]))
        loads.append(pltpu.make_async_copy(
            w_out_ref.at[:, cols], wout8.at[pl.ds(h * neurons, neurons)], load_sem.at[2, h]))
    for copy in loads[0::3] + loads[1::3] + loads[2::3]:
        copy.start()

    barrier = pltpu.get_barrier_semaphore()
    for k in range(1, n):
        pl.semaphore_signal(barrier, inc=1, device_id={"blk": lax.rem(me + k, n)},
                            device_id_type=pl.DeviceIdType.MESH)

    ids = ids_ref[...]
    block = iota((tok_dev, lanes), 1)
    member = jnp.zeros((tok_dev, lanes), F32)
    for k in range(top):
        member = member + (ids[:, k:k + 1] == block).astype(F32)
    lower = (iota((tok_dev, tok_dev), 1) < iota((tok_dev, tok_dev), 0)).astype(F32)
    rank = jnp.dot(lower, member, preferred_element_type=F32)
    rank = jnp.where(member > 0.5, rank, 99.0)
    rank8 = jnp.concatenate([rank] * PARTS, axis=0).astype(BF16)

    for copy in loads[0::3]:
        copy.wait()
    for g in range(n // group):
        row = iota((rows, lanes), 0)
        target = lax.rem(me + g * group + row // slab, n)
        pick = (target == iota((rows, lanes), 1)).astype(BF16)
        place = lax.dot_general(pick, rank8, (((1,), (1,)), ((), ())), preferred_element_type=F32)
        r = iota((rows, PARTS * tok_dev), 0) % slab
        c = iota((rows, PARTS * tok_dev), 1)
        chosen = (jnp.abs(place - (r % CAP).astype(F32)) < 0.5) & (r // CAP == c // tok_dev)
        chosen = chosen.astype(BF16)
        route[pl.ds(g * rows, rows), :] = chosen
        packed = jnp.dot(chosen, tok8[...], preferred_element_type=F32).astype(BF16)
        for i in range(group):
            outgoing[g * group + i] = packed[i * slab:(i + 1) * slab]
        if g == 0:
            pl.semaphore_wait(barrier, n - 1)
        for i in range(group):
            k = g * group + i
            if k > 0:
                pltpu.make_async_remote_copy(
                    src_ref=outgoing.at[k], dst_ref=incoming.at[k],
                    send_sem=fsend.at[k], recv_sem=frecv.at[k],
                    device_id={"blk": lax.rem(me + k, n)},
                    device_id_type=pl.DeviceIdType.MESH).start()

    for copy in loads[1::3] + loads[2::3]:
        copy.wait()
    ra, rb = iota((rows, rows), 0), iota((rows, rows), 1)
    same = ((ra // slab == rb // slab) & (ra % CAP == rb % CAP)).astype(F32)
    part = (iota((rows, PARTS * neurons), 0) % slab // CAP) == (
        iota((rows, PARTS * neurons), 1) // neurons)
    for g in range(n // group):
        slabs = []
        for i in range(group):
            k = g * group + i
            if k == 0:
                slabs.append(outgoing[0])
            else:
                pltpu.make_async_remote_copy(
                    src_ref=outgoing.at[k], dst_ref=incoming.at[k],
                    send_sem=fsend.at[k], recv_sem=frecv.at[k],
                    device_id={"blk": lax.rem(me + k, n)},
                    device_id_type=pl.DeviceIdType.MESH).wait_recv()
                slabs.append(incoming[k])
        x = jnp.concatenate(slabs, axis=0)
        wide = jnp.where(part, jnp.dot(x, win8[...], preferred_element_type=F32), 0.0)
        own = wide[:, :neurons]
        for h in range(1, PARTS):
            own = own + wide[:, h * neurons:(h + 1) * neurons]
        pre = jnp.dot(same, own, preferred_element_type=F32, precision=lax.Precision.HIGHEST)
        hidden = jnp.maximum(pre + bias_ref[...], 0.0)
        hidden8 = jnp.where(part, jnp.concatenate([hidden] * PARTS, axis=1), 0.0).astype(BF16)
        back = jnp.dot(hidden8, wout8[...], preferred_element_type=F32).astype(BF16)
        for i in range(group):
            k = g * group + i
            if k == 0:
                returned[0] = back[:slab]
            else:
                result[k] = back[i * slab:(i + 1) * slab]
        for i in range(group):
            k = g * group + i
            if k > 0:
                pltpu.make_async_remote_copy(
                    src_ref=result.at[k], dst_ref=returned.at[k],
                    send_sem=bsend.at[k], recv_sem=brecv.at[k],
                    device_id={"blk": lax.rem(me - k + n, n)},
                    device_id_type=pl.DeviceIdType.MESH).start()

    for g in range(n // group):
        slabs = []
        for i in range(group):
            k = g * group + i
            if k > 0:
                pltpu.make_async_remote_copy(
                    src_ref=result.at[k], dst_ref=returned.at[k],
                    send_sem=bsend.at[k], recv_sem=brecv.at[k],
                    device_id={"blk": lax.rem(me - k + n, n)},
                    device_id_type=pl.DeviceIdType.MESH).wait_recv()
            slabs.append(returned[k])
        y = jnp.concatenate(slabs, axis=0)
        total = lax.dot_general(route[pl.ds(g * rows, rows), :], y, (((0,), (0,)), ((), ())),
                                preferred_element_type=F32)
        if g == 0:
            acc[...] = total
        elif g < n // group - 1:
            acc[...] += total
        else:
            total = acc[...] + total
            for h in range(PARTS):
                out_ref[:, h * width:(h + 1) * width] = (
                    total[h * tok_dev:(h + 1) * tok_dev].astype(BF16))
    for k in range(1, n):
        pltpu.make_async_remote_copy(
            src_ref=outgoing.at[k], dst_ref=incoming.at[k],
            send_sem=fsend.at[k], recv_sem=frecv.at[k],
            device_id={"blk": lax.rem(me + k, n)},
            device_id_type=pl.DeviceIdType.MESH).wait_send()
        pltpu.make_async_remote_copy(
            src_ref=result.at[k], dst_ref=returned.at[k],
            send_sem=bsend.at[k], recv_sem=brecv.at[k],
            device_id={"blk": lax.rem(me - k + n, n)},
            device_id_type=pl.DeviceIdType.MESH).wait_send()


def body(tokens, block_ids, w_in, bias_in, w_out):
    n = lax.axis_size("blk")
    tok_dev, model_width = tokens.shape
    neurons = w_in.shape[1]
    width = model_width // PARTS
    slab = CAP * PARTS
    group = math.gcd(n, 4)
    return pl.pallas_call(
        functools.partial(kernel, n, group),
        out_shape=jax.ShapeDtypeStruct((tok_dev, model_width), BF16),
        in_specs=[
            pl.BlockSpec(memory_space=pl.ANY),
            pl.BlockSpec(memory_space=pltpu.VMEM),
            pl.BlockSpec(memory_space=pl.ANY),
            pl.BlockSpec(memory_space=pltpu.VMEM),
            pl.BlockSpec(memory_space=pl.ANY),
        ],
        out_specs=pl.BlockSpec(memory_space=pltpu.VMEM),
        scratch_shapes=[
            pltpu.VMEM((PARTS * tok_dev, width), BF16),
            pltpu.VMEM((width, PARTS * neurons), BF16),
            pltpu.VMEM((PARTS * neurons, width), BF16),
            pltpu.VMEM((n, slab, width), BF16),
            pltpu.VMEM((n, slab, width), BF16),
            pltpu.VMEM((n, slab, width), BF16),
            pltpu.VMEM((n, slab, width), BF16),
            pltpu.VMEM((n * slab, PARTS * tok_dev), BF16),
            pltpu.VMEM((PARTS * tok_dev, width), F32),
            pltpu.SemaphoreType.DMA((3, PARTS)),
            pltpu.SemaphoreType.DMA((n,)),
            pltpu.SemaphoreType.DMA((n,)),
            pltpu.SemaphoreType.DMA((n,)),
            pltpu.SemaphoreType.DMA((n,)),
        ],
        compiler_params=pltpu.CompilerParams(
            collective_id=0, has_side_effects=True, vmem_limit_bytes=60 * 1024 * 1024),
    )(tokens, block_ids, w_in, bias_in.reshape(1, -1), w_out)


def solution(mesh):
    return jax.shard_map(
        body,
        mesh=mesh,
        in_specs=(
            P(("tok", "blk"), None),
            P(("tok", "blk"), None),
            P(None, "blk"),
            P("blk"),
            P("blk", None),
        ),
        out_specs=P(("tok", "blk"), None),
        check_vma=False,
    )
```

time: 145 us -> 86.2 us (0.59)
  blocking collectives: 122 us -> 0 us
  Pallas kernels: 0 us -> 83 us
  local copies, waits for them, and re-layouts: 12.6 us -> 3.05 us
  matrix products: 9.4 us -> 0 us
    all_to_all x2 -> x0, blocking collectives: 122 us -> none  [the longest x1 63.4 us: body(): lax.all_to_all(outgoing, 'blk', split_axis=0, concat_axis=0, tiled=True)]
    pallas_call x0 -> x1, Pallas kernels: none -> 83 us  [body(): pl.pallas_call(functools.partial(kernel, n, group), out_shape=jax.ShapeDt...]
    reshape x4 -> x0, local copies, waits for them, and re-layouts: 11.4 us -> none  [the longest x1 2.86 us: body(): outgoing = outgoing.reshape(peer_count, CAP, model_width)]
    dot_general x3 -> x0, matrix products: 9.4 us -> none  [the longest x1 4.33 us: body(): jnp.dot(hidden, w_out, preferred_element_type=jnp.float32)]
    unnamed x5 -> x2, local copies, waits for them, and re-layouts: 0.91 us -> 3.05 us
where the time goes in v1:
time: 86.2 us; the launch traced here: 86 us
  Pallas kernels  83 us (96%)
  local copies, waits for them, and re-layouts  3.05 us (4%)
    pallas_call x1, Pallas kernels, body(): pl.pallas_call(functools.partial(kernel, n, group), out_shape=jax.ShapeDt...  83 us
    unnamed x2, local copies, waits for them, and re-layouts  3.05 us

profile of v1, /device:TPU:0, one launch (start us, length us, event | category | flops | bytes accessed | tf_op | source)
XLA Modules:
  0.0 86.0 jit_solution(609158862714667943)
XLA Ops:
  0.0 1.4 %copy.6.ids_ref = s32[16,2]{1,0:T(8,128)} copy(s32[16,2]{0,1:T(2,128)} %param.6) | data formatting | bytes 256 | tf_op args[1]
  1.4 83.0 %shard_map.55 = bf16[16,9216]{1,0:T(8,128)(2,1)} custom-call(bf16[16,9216]{1,0:T(8,128)(2,1)} %tok_ref.1, s32[16,2]{1,0:T(8,128)} %copy.6.ids_ref, bf16[9216,128]{1,0:T(8,128)(2,1)} %w_in_ref.1, f32[1,128]{1,0:T(1,128)} %bitcast.1, bf16[128,9216]{1,0:T(8,128)(2,1)} %w_out_ref.1), custom_call_target="tpu_custom_call" | custom-call | tf_op jit(solution)/shard_map/pallas_call | solution.py:173
  84.3 1.7 %copy.8 = bf16[16,9216]{1,0:T(8,128)(2,1)} copy(bf16[16,9216]{1,0:T(8,128)(2,1)} %shard_map.55) | data formatting | bytes 589824

commit v2 on v0

v2 whole, which is shorter than its diff:
```python
import functools
import math

import jax
import jax.numpy as jnp
from jax import lax
from jax.experimental import pallas as pl
from jax.experimental.pallas import tpu as pltpu
from jax.sharding import PartitionSpec as P

CAP = 5
PARTS = 8
CHUNKS = 4
F32 = jnp.float32
BF16 = jnp.bfloat16


def iota(shape, dim):
    return lax.broadcasted_iota(jnp.int32, shape, dim)


def lookup(index, values):
    total = values[0]
    for at, value in enumerate(values):
        total = jnp.where(index == at, value, total)
    return total


def remote(src, dst, send, recv, target):
    return pltpu.make_async_remote_copy(
        src_ref=src, dst_ref=dst, send_sem=send, recv_sem=recv,
        device_id={"blk": target}, device_id_type=pl.DeviceIdType.MESH)


def kernel(
    outer, inner, tok_ref, ids_ref, w_in_ref, bias_ref, w_out_ref, out_ref,
    raw, ranks, win8, wout8, outgoing, incoming, result, returned, route, partial, above, below, acc,
    load_sem, raw_send, raw_recv, rank_send, rank_recv, fsend, frecv, bsend, brecv,
    part_send, above_recv, below_recv,
):
    me = lax.axis_index("blk")
    o, i0 = me // inner, me % inner
    last = outer - 1
    tok_dev, top = ids_ref.shape
    width = raw.shape[2]
    neurons = w_in_ref.shape[1]
    lanes = ranks.shape[2]
    slab = CAP * PARTS
    rows = inner * slab
    piece = PARTS * tok_dev // CHUNKS

    near = [sorted(range(outer), key=lambda s, a=a: (abs(s - a), s)) for a in range(outer)]
    ready = [sorted([s for s in range(outer) if s != a],
                    key=lambda s, a=a: (s + a if s > a else 2 * last - s - a, s))
             for a in range(outer)]
    source = [lookup(o, [near[a][t] for a in range(outer)]) for t in range(outer)]

    loads = []
    for h in range(PARTS):
        cols = pl.ds(h * width, width)
        loads.append(pltpu.make_async_copy(
            tok_ref.at[:, cols], raw.at[o, pl.ds(h * tok_dev, tok_dev)], load_sem.at[0, h]))
        loads.append(pltpu.make_async_copy(
            w_in_ref.at[cols], win8.at[:, pl.ds(h * neurons, neurons)], load_sem.at[1, h]))
        loads.append(pltpu.make_async_copy(
            w_out_ref.at[:, cols], wout8.at[pl.ds(h * neurons, neurons)], load_sem.at[2, h]))
    for copy in loads[0::3] + loads[1::3] + loads[2::3]:
        copy.start()

    column = [lax.rem(o + k, outer) * inner + i0 for k in range(outer)]
    ahead = [o * inner + lax.rem(i0 + k, inner) for k in range(inner)]
    behind = [o * inner + lax.rem(i0 - k + inner, inner) for k in range(inner)]
    barrier = pltpu.get_barrier_semaphore()
    for target in column[1:] + ahead[1:]:
        pl.semaphore_signal(barrier, inc=1, device_id={"blk": target},
                            device_id_type=pl.DeviceIdType.MESH)

    ids = ids_ref[...]
    block = iota((tok_dev, lanes), 1)
    member = jnp.zeros((tok_dev, lanes), F32)
    for k in range(top):
        member = member + (ids[:, k:k + 1] == block).astype(F32)
    lower = (iota((tok_dev, tok_dev), 1) < iota((tok_dev, tok_dev), 0)).astype(F32)
    rank = jnp.dot(lower, member, preferred_element_type=F32)
    ranks[o] = jnp.where(member > 0.5, rank, 99.0).astype(BF16)

    up = jnp.minimum(o + 1, last) * inner + i0
    down = jnp.maximum(o - 1, 0) * inner + i0

    def raw_copy(s, side):
        return remote(raw.at[s], raw.at[s], raw_send.at[side, s], raw_recv.at[s],
                      up if side == 0 else down)

    def rank_copy(k, s):
        return remote(ranks.at[s], ranks.at[s], rank_send.at[k], rank_recv.at[s], column[k])

    def out_copy(t, k):
        return remote(outgoing.at[t, k], incoming.at[t, k], fsend.at[t, k], frecv.at[t, k], ahead[k])

    def back_copy(t, k):
        return remote(result.at[t, k], returned.at[t, k], bsend.at[t, k], brecv.at[t, k], behind[k])

    def part_copy(s, c, side):
        span = pl.ds(c * piece, piece)
        land, recv = (below, below_recv) if side == 0 else (above, above_recv)
        return remote(partial.at[s, span], land.at[s, span], part_send.at[s, c], recv.at[s, c],
                      up if side == 0 else down)

    row = iota((rows, lanes), 0)
    pick = ((o * inner + (i0 + row // slab) % inner) == iota((rows, lanes), 1)).astype(BF16)
    r = iota((rows, PARTS * tok_dev), 0) % slab
    slot = (r % CAP).astype(F32)
    aligned = r // CAP == iota((rows, PARTS * tok_dev), 1) // tok_dev
    ra, rb = iota((rows, rows), 0), iota((rows, rows), 1)
    same = ((ra // slab == rb // slab) & (ra % CAP == rb % CAP)).astype(F32)
    part = (iota((rows, PARTS * neurons), 0) % slab // CAP) == (
        iota((rows, PARTS * neurons), 1) // neurons)

    def dispatch(t):
        s = source[t]
        if t > 0:
            raw_copy(s, 0).wait_recv()

        @pl.when((s <= o) & (o < last))
        def _():
            raw_copy(s, 0).start()

        @pl.when((s >= o) & (o > 0))
        def _():
            raw_copy(s, 1).start()

        if t == 0:
            for k in range(1, outer):
                rank_copy(k, o).start()
        else:
            rank_copy(0, s).wait_recv()
        rank8 = jnp.concatenate([ranks[s]] * PARTS, axis=0)
        place = lax.dot_general(pick, rank8, (((1,), (1,)), ((), ())), preferred_element_type=F32)
        chosen = ((jnp.abs(place - slot) < 0.5) & aligned).astype(BF16)
        route[t] = chosen
        packed = jnp.dot(chosen, raw[s], preferred_element_type=F32).astype(BF16)
        for k in range(inner):
            outgoing[t, k] = packed[k * slab:(k + 1) * slab]
        for k in range(1, inner):
            out_copy(t, k).start()

    def compute(t):
        for k in range(1, inner):
            out_copy(t, k).wait_recv()
        x = jnp.concatenate([outgoing[t, 0]] + [incoming[t, k] for k in range(1, inner)], axis=0)
        wide = jnp.where(part, jnp.dot(x, win8[...], preferred_element_type=F32), 0.0)
        own = wide[:, :neurons]
        for h in range(1, PARTS):
            own = own + wide[:, h * neurons:(h + 1) * neurons]
        pre = jnp.dot(same, own, preferred_element_type=F32, precision=lax.Precision.HIGHEST)
        hidden = jnp.maximum(pre + bias_ref[...], 0.0)
        hidden8 = jnp.where(part, jnp.concatenate([hidden] * PARTS, axis=1), 0.0).astype(BF16)
        back = jnp.dot(hidden8, wout8[...], preferred_element_type=F32).astype(BF16)
        for k in range(inner):
            result[t, k] = back[k * slab:(k + 1) * slab]
        for k in range(1, inner):
            back_copy(t, k).start()

    def pass_on(s, wait):
        for side in range(2):
            land, recv = (below, below_recv) if side == 0 else (above, above_recv)

            @pl.when((s > o) if side == 0 else (s < o))
            def _():
                for c in range(CHUNKS):
                    span = pl.ds(c * piece, piece)
                    if wait:
                        part_copy(s, c, side).wait_recv()
                        partial[s, span] = (
                            partial[s, span].astype(F32) + land[s, span].astype(F32)).astype(BF16)
                    part_copy(s, c, side).start()

    def combine(t):
        for k in range(1, inner):
            back_copy(t, k).wait_recv()
        y = jnp.concatenate([result[t, 0]] + [returned[t, k] for k in range(1, inner)], axis=0)
        total = lax.dot_general(route[t], y, (((0,), (0,)), ((), ())), preferred_element_type=F32)
        s = source[t]
        partial[s] = total.astype(BF16)
        if t > 0:
            @pl.when((o == 0) | (o == last))
            def _():
                pass_on(s, False)

    for copy in loads[0::3]:
        copy.wait()
    pl.semaphore_wait(barrier, outer + inner - 2)
    for t in range(outer + 2):
        if t < outer:
            dispatch(t)
        if t == 1:
            for copy in loads[1::3] + loads[2::3]:
                copy.wait()
        if 1 <= t <= outer:
            compute(t - 1)
        if t >= 2:
            combine(t - 2)

    for t in range(outer - 1):
        s = lookup(o, [ready[a][t] for a in range(outer)])

        @pl.when((o > 0) & (o < last))
        def _():
            pass_on(s, True)

    for c in range(CHUNKS):
        span = pl.ds(c * piece, piece)
        acc[...] = partial[o, span].astype(F32)

        @pl.when(o < last)
        def _():
            part_copy(o, c, 1).wait_recv()
            acc[...] += above[o, span].astype(F32)

        @pl.when(o > 0)
        def _():
            part_copy(o, c, 0).wait_recv()
            acc[...] += below[o, span].astype(F32)

        for j in range(PARTS // CHUNKS):
            h = c * (PARTS // CHUNKS) + j
            out_ref[:, h * width:(h + 1) * width] = (
                acc[j * tok_dev:(j + 1) * tok_dev].astype(BF16))

    for t in range(outer):
        s = source[t]

        @pl.when((s <= o) & (o < last))
        def _():
            raw_copy(s, 0).wait_send()

        @pl.when((s >= o) & (o > 0))
        def _():
            raw_copy(s, 1).wait_send()

        for k in range(1, inner):
            out_copy(t, k).wait_send()
            back_copy(t, k).wait_send()
        if t > 0:
            rank_copy(t, o).wait_send()
            for c in range(CHUNKS):
                part_copy(s, c, 0).wait_send()


def body(tokens, block_ids, w_in, bias_in, w_out):
    n = lax.axis_size("blk")
    tok_dev, model_width = tokens.shape
    neurons = w_in.shape[1]
    width = model_width // PARTS
    slab = CAP * PARTS
    inner = max(k for k in range(1, math.isqrt(n) + 1) if n % k == 0)
    outer = n // inner
    lanes = 128 * ((n + 127) // 128)
    lines = pltpu.VMEM((outer, PARTS * tok_dev, width), BF16)
    slabs = pltpu.VMEM((outer, inner, slab, width), BF16)
    dma = pltpu.SemaphoreType.DMA
    return pl.pallas_call(
        functools.partial(kernel, outer, inner),
        out_shape=jax.ShapeDtypeStruct((tok_dev, model_width), BF16),
        in_specs=[
            pl.BlockSpec(memory_space=pl.ANY),
            pl.BlockSpec(memory_space=pltpu.VMEM),
            pl.BlockSpec(memory_space=pl.ANY),
            pl.BlockSpec(memory_space=pltpu.VMEM),
            pl.BlockSpec(memory_space=pl.ANY),
        ],
        out_specs=pl.BlockSpec(memory_space=pltpu.VMEM),
        scratch_shapes=[
            lines,
            pltpu.VMEM((outer, tok_dev, lanes), BF16),
            pltpu.VMEM((width, PARTS * neurons), BF16),
            pltpu.VMEM((PARTS * neurons, width), BF16),
            slabs, slabs, slabs, slabs,
            pltpu.VMEM((outer, inner * slab, PARTS * tok_dev), BF16),
            lines, lines, lines,
            pltpu.VMEM((PARTS * tok_dev // CHUNKS, width), F32),
            dma((3, PARTS)),
            dma((2, outer)), dma((outer,)),
            dma((outer,)), dma((outer,)),
            dma((outer, inner)), dma((outer, inner)),
            dma((outer, inner)), dma((outer, inner)),
            dma((outer, CHUNKS)), dma((outer, CHUNKS)), dma((outer, CHUNKS)),
        ],
        compiler_params=pltpu.CompilerParams(
            collective_id=0, has_side_effects=True, vmem_limit_bytes=60 * 1024 * 1024),
    )(tokens, block_ids, w_in, bias_in.reshape(1, -1), w_out)


def solution(mesh):
    return jax.shard_map(
        body,
        mesh=mesh,
        in_specs=(
            P(("tok", "blk"), None),
            P(("tok", "blk"), None),
            P(None, "blk"),
            P("blk"),
            P("blk", None),
        ),
        out_specs=P(("tok", "blk"), None),
        check_vma=False,
    )
```

time: 145 us -> 65.2 us (0.45)
  blocking collectives: 122 us -> 0 us
  Pallas kernels: 0 us -> 61.9 us
  local copies, waits for them, and re-layouts: 12.6 us -> 3.05 us
  matrix products: 9.4 us -> 0 us
    all_to_all x2 -> x0, blocking collectives: 122 us -> none  [the longest x1 63.4 us: body(): lax.all_to_all(outgoing, 'blk', split_axis=0, concat_axis=0, tiled=True)]
    pallas_call x0 -> x1, Pallas kernels: none -> 61.9 us  [body(): pl.pallas_call(functools.partial(kernel, outer, inner), out_shape=jax.Sha...]
    reshape x4 -> x0, local copies, waits for them, and re-layouts: 11.4 us -> none  [the longest x1 2.86 us: body(): outgoing = outgoing.reshape(peer_count, CAP, model_width)]
    dot_general x3 -> x0, matrix products: 9.4 us -> none  [the longest x1 4.33 us: body(): jnp.dot(hidden, w_out, preferred_element_type=jnp.float32)]
    unnamed x5 -> x2, local copies, waits for them, and re-layouts: 0.91 us -> 3.05 us
where the time goes in v2:
time: 65.2 us; the launch traced here: 65 us
  Pallas kernels  61.9 us (95%)
  local copies, waits for them, and re-layouts  3.05 us (5%)
    pallas_call x1, Pallas kernels, body(): pl.pallas_call(functools.partial(kernel, outer, inner), out_shape=jax.Sha...  61.9 us
    unnamed x2, local copies, waits for them, and re-layouts  3.05 us

profile of v2, /device:TPU:0, one launch (start us, length us, event | category | flops | bytes accessed | tf_op | source)
XLA Modules:
  0.0 65.0 jit_solution(1706913618529493051)
XLA Ops:
  0.0 1.4 %copy.6.ids_ref = s32[16,2]{1,0:T(8,128)} copy(s32[16,2]{0,1:T(2,128)} %param.6) | data formatting | bytes 256 | tf_op args[1]
  1.4 61.9 %shard_map.55 = bf16[16,9216]{1,0:T(8,128)(2,1)} custom-call(bf16[16,9216]{1,0:T(8,128)(2,1)} %tok_ref.1, s32[16,2]{1,0:T(8,128)} %copy.6.ids_ref, bf16[9216,128]{1,0:T(8,128)(2,1)} %w_in_ref.1, f32[1,128]{1,0:T(1,128)} %bitcast.1, bf16[128,9216]{1,0:T(8,128)(2,1)} %w_out_ref.1), custom_call_target="tpu_custom_call" | custom-call | tf_op jit(solution)/shard_map/pallas_call | solution.py:262
  63.3 1.7 %copy.8 = bf16[16,9216]{1,0:T(8,128)(2,1)} copy(bf16[16,9216]{1,0:T(8,128)(2,1)} %shard_map.55) | data formatting | bytes 589824

commit v3 on v2

--- a/solution.py
+++ b/solution.py
@@ -41,7 +41,7 @@
     me = lax.axis_index("blk")
     o, i0 = me // inner, me % inner
     last = outer - 1
-    tok_dev, top = ids_ref.shape
+    top, tok_dev = ids_ref.shape
     width = raw.shape[2]
     neurons = w_in_ref.shape[1]
     lanes = ranks.shape[2]
@@ -54,6 +54,14 @@
                     key=lambda s, a=a: (s + a if s > a else 2 * last - s - a, s))
              for a in range(outer)]
     source = [lookup(o, [near[a][t] for a in range(outer)]) for t in range(outer)]
+
+    column = [lax.rem(o + k, outer) * inner + i0 for k in range(outer)]
+    ahead = [o * inner + lax.rem(i0 + k, inner) for k in range(inner)]
+    behind = [o * inner + lax.rem(i0 - k + inner, inner) for k in range(inner)]
+    barrier = pltpu.get_barrier_semaphore()
+    for target in column[1:] + ahead[1:]:
+        pl.semaphore_signal(barrier, inc=1, device_id={"blk": target},
+                            device_id_type=pl.DeviceIdType.MESH)
 
     loads = []
     for h in range(PARTS):
@@ -67,22 +75,17 @@
     for copy in loads[0::3] + loads[1::3] + loads[2::3]:
         copy.start()
 
-    column = [lax.rem(o + k, outer) * inner + i0 for k in range(outer)]
-    ahead = [o * inner + lax.rem(i0 + k, inner) for k in range(inner)]
-    behind = [o * inner + lax.rem(i0 - k + inner, inner) for k in range(inner)]
-    barrier = pltpu.get_barrier_semaphore()
-    for target in column[1:] + ahead[1:]:
-        pl.semaphore_signal(barrier, inc=1, device_id={"blk": target},
-                            device_id_type=pl.DeviceIdType.MESH)
-
     ids = ids_ref[...]
-    block = iota((tok_dev, lanes), 1)
-    member = jnp.zeros((tok_dev, lanes), F32)
+    block = iota((lanes, tok_dev), 0)
+    member = jnp.zeros((lanes, tok_dev), F32)
     for k in range(top):
-        member = member + (ids[:, k:k + 1] == block).astype(F32)
-    lower = (iota((tok_dev, tok_dev), 1) < iota((tok_dev, tok_dev), 0)).astype(F32)
-    rank = jnp.dot(lower, member, preferred_element_type=F32)
-    ranks[o] = jnp.where(member > 0.5, rank, 99.0).astype(BF16)
+        member = member + (ids[k:k + 1, :] == block).astype(F32)
+    earlier = (iota((tok_dev, tok_dev), 0) < iota((tok_dev, tok_dev), 1)).astype(F32)
+    rank = jnp.dot(member, earlier, preferred_element_type=F32)
+    rank = jnp.where(member > 0.5, rank, 99.0).astype(BF16)
+    unit = (iota((lanes, lanes), 0) == iota((lanes, lanes), 1)).astype(BF16)
+    ranks[o] = lax.dot_general(rank, unit, (((0,), (0,)), ((), ())),
+                               preferred_element_type=F32).astype(BF16)
 
     up = jnp.minimum(o + 1, last) * inner + i0
     down = jnp.maximum(o - 1, 0) * inner + i0
@@ -116,23 +119,40 @@
     part = (iota((rows, PARTS * neurons), 0) % slab // CAP) == (
         iota((rows, PARTS * neurons), 1) // neurons)
 
+    inside = (o > 0) & (o < last)
+
+    def relay(t):
+        @pl.when(inside)
+        def _():
+            s = source[t]
+            raw_copy(s, 0).wait_recv()
+
+            @pl.when(s < o)
+            def _():
+                raw_copy(s, 0).start()
+
+            @pl.when(s > o)
+            def _():
+                raw_copy(s, 1).start()
+
     def dispatch(t):
         s = source[t]
-        if t > 0:
-            raw_copy(s, 0).wait_recv()
-
-        @pl.when((s <= o) & (o < last))
-        def _():
-            raw_copy(s, 0).start()
-
-        @pl.when((s >= o) & (o > 0))
-        def _():
-            raw_copy(s, 1).start()
-
         if t == 0:
+            @pl.when(o < last)
+            def _():
+                raw_copy(o, 0).start()
+
+            @pl.when(o > 0)
+            def _():
+                raw_copy(o, 1).start()
+
             for k in range(1, outer):
                 rank_copy(k, o).start()
         else:
+            @pl.when(jnp.logical_not(inside))
+            def _():
+                raw_copy(s, 0).wait_recv()
+
             rank_copy(0, s).wait_recv()
         rank8 = jnp.concatenate([ranks[s]] * PARTS, axis=0)
         place = lax.dot_general(pick, rank8, (((1,), (1,)), ((), ())), preferred_element_type=F32)
@@ -183,7 +203,7 @@
         s = source[t]
         partial[s] = total.astype(BF16)
         if t > 0:
-            @pl.when((o == 0) | (o == last))
+            @pl.when(jnp.logical_not(inside))
             def _():
                 pass_on(s, False)
 
@@ -191,9 +211,11 @@
         copy.wait()
     pl.semaphore_wait(barrier, outer + inner - 2)
     for t in range(outer + 2):
+        if 0 < t < outer:
+            relay(t)
         if t < outer:
             dispatch(t)
-        if t == 1:
+        if t == 0:
             for copy in loads[1::3] + loads[2::3]:
                 copy.wait()
         if 1 <= t <= outer:
@@ -204,7 +226,7 @@
     for t in range(outer - 1):
         s = lookup(o, [ready[a][t] for a in range(outer)])
 
-        @pl.when((o > 0) & (o < last))
+        @pl.when(inside)
         def _():
             pass_on(s, True)
 
@@ -288,7 +310,7 @@
         ],
         compiler_params=pltpu.CompilerParams(
             collective_id=0, has_side_effects=True, vmem_limit_bytes=60 * 1024 * 1024),
-    )(tokens, block_ids, w_in, bias_in.reshape(1, -1), w_out)
+    )(tokens, block_ids.T, w_in, bias_in.reshape(1, -1), w_out)
 
 
 def solution(mesh):

time: 65.2 us -> 63.7 us (0.977)
  local copies, waits for them, and re-layouts: 3.05 us -> 1.69 us
    unnamed x2 -> x1, local copies, waits for them, and re-layouts: 3.05 us -> 1.69 us
where the time goes in v3:
time: 63.7 us; the launch traced here: 63.5 us
  Pallas kernels  61.8 us (97%)
  local copies, waits for them, and re-layouts  1.69 us (3%)
    pallas_call x1, Pallas kernels, body(): pl.pallas_call(functools.partial(kernel, outer, inner), out_shape=jax.Sha...  61.8 us
    unnamed x1, local copies, waits for them, and re-layouts  1.69 us

profile of v3, /device:TPU:0, one launch (start us, length us, event | category | flops | bytes accessed | tf_op | source)
XLA Modules:
  0.0 63.5 jit_solution(2056075511381640373)
XLA Ops:
  0.0 61.8 %shard_map.55 = bf16[16,9216]{1,0:T(8,128)(2,1)} custom-call(bf16[16,9216]{1,0:T(8,128)(2,1)} %tok_ref.1, s32[2,16]{1,0:T(2,128)} %bitcast.2, bf16[9216,128]{1,0:T(8,128)(2,1)} %w_in_ref.1, f32[1,128]{1,0:T(1,128)} %bitcast.3, bf16[128,9216]{1,0:T(8,128)(2,1)} %w_out_ref.1), custom_call_target="tpu_custom_call" | custom-call | tf_op jit(solution)/shard_map/pallas_call | solution.py:284
  61.8 1.7 %copy.7 = bf16[16,9216]{1,0:T(8,128)(2,1)} copy(bf16[16,9216]{1,0:T(8,128)(2,1)} %shard_map.55) | data formatting | bytes 589824
